TPU v7x, 256 devices: a whole 4x4x8 slice. The times are simulated.
256 devices in a mesh: dp: 32 (over y, x, core), ind: 8 (over z).
Axes of the slice: x: 4, y: 4, z: 8, core: 2. Of those that a mesh axis runs over, the one named last changes fastest.
Arguments:
- inputs: bfloat16 [65536, 256], P('dp'), may hold values from -6 to 6
- targets: bfloat16 [65536], P('dp'), may hold values from -6 to 6
- row_counts: int32 [32], replicated, may hold values from 1 to 2048, 32768 in all
- w_in: bfloat16 [256, 1024], replicated, may hold values from -0.375 to 0.375
- w_mid: bfloat16 [1024, 1024], replicated, may hold values from -0.1875 to 0.1875
- w_out: bfloat16 [1024, 128], replicated, may hold values from -0.1875 to 0.1875
- feat_gain: float32 [128], replicated, may hold values from 0.1 to 1.9
- inducing: bfloat16 [16384, 128], P('ind'), may hold values from -6 to 6
- log_scale: float32 [1], replicated, may hold values from -0.5 to 0.5
- lengthscale: float32 [1], replicated, may hold values from 3.2 to 3.5
- noise_var: float32 [1], replicated, may hold values from 5e-05 to 0.0002
Outputs:
- panel_factor: float32 [16384, 512], P(('ind', 'dp'))
- rhs_next: float32 [16384], P(('ind', 'dp'))
- panel_solution: float32 [512], replicated
- log_det: float32 [1], replicated
Inputs may be any that keep to these rules, and one draw needn't show every extreme that they name: The first row_counts[s] samples of shard s are valid; the counts sum to 32768 and one shard has all 2048 slots valid.
All inputs are finite; a program needn't handle non-finite values.
Results may differ from a plain program's by a relative error of at most 0.012.
The roundings to bfloat16 on the way count: a program that leaves them out, or rounds other values in their place, can miss the bound.
Values may be sent and summed in bfloat16 or wider, within the bound.
No kernel may reach another device: no remote copies, remote signals or barrier semaphores. Data moves between devices by JAX's collectives and lax.ppermute only.
A program may use at most 64 MiB of HBM per device.

v0:
```python
import jax
import jax.numpy as jnp
from jax import lax
from jax.sharding import PartitionSpec as P

PB = 512
JITTER = 0.0001


def from_root(shard, axis, root):
    mine = lax.axis_index(axis) == root
    return lax.psum(jnp.where(mine, shard, jnp.zeros_like(shard)), axis)


def embed(inputs, w_in, w_mid, w_out, feat_gain):
    hidden_one = jax.nn.gelu(jnp.dot(inputs, w_in, preferred_element_type=jnp.float32)).astype(
        jnp.bfloat16
    )
    hidden_two = jax.nn.gelu(jnp.dot(hidden_one, w_mid, preferred_element_type=jnp.float32)).astype(
        jnp.bfloat16
    )
    projected = jnp.dot(hidden_two, w_out, preferred_element_type=jnp.float32)
    scaled = (
        projected
        * lax.rsqrt(jnp.mean(projected * projected, axis=-1, keepdims=True) + 1e-06)
        * feat_gain
    )
    return scaled.astype(jnp.bfloat16)


def exponent(points, others, scale_log, inverse_sq):
    point_sq = jnp.sum(jnp.square(points.astype(jnp.float32)), axis=1)
    other_sq = jnp.sum(jnp.square(others.astype(jnp.float32)), axis=1)
    cross_term = jnp.dot(points, others.T, preferred_element_type=jnp.float32)
    return (
        scale_log
        - 0.5 * inverse_sq * (point_sq[:, None] + other_sq[None, :])
        + inverse_sq * cross_term
    )


def body(
    inputs,
    targets,
    row_counts,
    w_in,
    w_mid,
    w_out,
    feat_gain,
    inducing,
    log_scale,
    lengthscale,
    noise_var,
):
    shards = lax.axis_size("dp")
    groups = lax.axis_size("ind")
    shard_id = lax.axis_index("dp")
    group_id = lax.axis_index("ind")
    capacity = inputs.shape[0]
    piece_rows = capacity // groups
    block_rows = inducing.shape[0]
    owned_rows = block_rows // shards
    start_row = group_id * piece_rows
    input_piece = lax.dynamic_slice_in_dim(inputs, start_row, piece_rows, 0)
    embedded_piece = embed(input_piece, w_in, w_mid, w_out, feat_gain)
    shard_iota = jnp.arange(shards, dtype=jnp.int32)
    own_count = jnp.sum(jnp.where(shard_iota == shard_id, row_counts, 0))
    embedded = lax.all_gather(embedded_piece, "ind", axis=0, tiled=True)
    valid_rows = jnp.arange(capacity, dtype=jnp.int32) < own_count
    target_used = jnp.where(valid_rows, targets, jnp.zeros((), jnp.bfloat16))
    scale_log = log_scale[0]
    inverse_sq = 1.0 / (lengthscale[0] * lengthscale[0])
    variance = noise_var[0]
    panel_points = from_root(inducing[:PB], "ind", 0)
    panel_kernel = jnp.where(
        valid_rows[None, :], jnp.exp(exponent(panel_points, embedded, scale_log, inverse_sq)), 0.0
    ).astype(jnp.bfloat16)
    block_size = min(512, block_rows)
    grouped = inducing.reshape(block_rows // block_size, block_size, inducing.shape[1])

    def gram_block(points):
        kernel_rows = jnp.exp(exponent(points, embedded, scale_log, inverse_sq)).astype(
            jnp.bfloat16
        )
        return (
            jnp.dot(kernel_rows, panel_kernel.T, preferred_element_type=jnp.float32),
            jnp.dot(kernel_rows, target_used, preferred_element_type=jnp.float32),
        )

    gram_rows, cross_rows = lax.map(gram_block, grouped)
    gram_rows = gram_rows.reshape(block_rows, gram_rows.shape[2])
    cross_rows = cross_rows.reshape(block_rows)
    gram_total, cross_total = lax.psum((gram_rows, cross_rows), "dp")
    gram_own = lax.dynamic_slice_in_dim(gram_total, shard_id * owned_rows, owned_rows, 0)
    cross_own = lax.dynamic_slice_in_dim(cross_total, shard_id * owned_rows, owned_rows, 0)
    own_index = (
        group_id * block_rows + shard_id * owned_rows + jnp.arange(owned_rows, dtype=jnp.int32)
    )
    panel_index = jnp.arange(PB, dtype=jnp.int32)
    own_points = lax.dynamic_slice_in_dim(inducing, shard_id * owned_rows, owned_rows, 0)
    kernel_mm = jnp.exp(exponent(own_points, panel_points, scale_log, inverse_sq)) + jnp.where(
        own_index[:, None] == panel_index[None, :], JITTER, 0.0
    )
    system_rows = kernel_mm + gram_own / variance
    right_side = cross_own / variance
    column_rows, column_right = (
        lax.all_gather(system_rows, "dp", axis=0, tiled=True),
        lax.all_gather(right_side, "dp", axis=0, tiled=True),
    )
    system_top, right_top = (
        from_root(column_rows[:PB], "ind", 0),
        from_root(column_right[:PB], "ind", 0),
    )
    factor_top = jnp.linalg.cholesky(system_top)
    log_det = 2.0 * jnp.sum(jnp.log(jnp.diagonal(factor_top)))
    panel_solution = lax.linalg.triangular_solve(
        factor_top, right_top[:, None], left_side=True, lower=True
    )[:, 0]
    panel_factor = lax.linalg.triangular_solve(
        factor_top, system_rows, left_side=False, lower=True, transpose_a=True
    )
    rhs_next = right_side - jnp.dot(panel_factor, panel_solution, precision=lax.Precision.HIGHEST)
    return (panel_factor, rhs_next, panel_solution, log_det.reshape(1))


def solution(mesh):
    return jax.shard_map(
        body,
        mesh=mesh,
        in_specs=(P("dp", None), P("dp"), P(), P(), P(), P(), P(), P("ind", None), P(), P(), P()),
        out_specs=(P(("ind", "dp"), None), P(("ind", "dp")), P(), P()),
        check_vma=False,
    )
```

profile of v0, /device:TPU:0, one launch (start us, length us, event | category | flops | bytes accessed | tf_op | source)
XLA Modules:
  0.0 630.5 jit_solution(4431157111453220107)
XLA Ops:
  7.2 1.7 slice_select_fusion
  9.0 1.4 fusion.56
  10.5 2.1 multiply_reduce_fusion.4
  12.7 27.6 %all_gather.9 = bf16[2048,128]{0,1:T(8,128)(2,1)S(1)} all-gather(bf16[256,128]{0,1:T(8,128)(2,1)S(1)} %multiply_convert_fusion), channel_id=1, replica_groups=mesh['dp'=32,'ind'=8] {'ind'}, dimensions={0}, use_global_device_ids=true | all-gather | bytes 589824 | tf_op jit(solution)/shard_map/all_gather | solution.py:68
  44.0 40.7 %all-reduce.6.cloned.1.call-done = bf16[512,128]{1,0:T(8,128)(2,1)} async-done(((bf16[512,128]{1,0:T(8,128)(2,1)}), bf16[512,128]{1,0:T(8,128)(2,1)}) %all-reduce.6.cloned.1.call-update) | async-done | bytes 131088 | tf_op jit(solution)/shard_map/psum | solution.py:12
  84.8 1.0 multiply_reduce_fusion.3
  85.8 3.6 select_convert_fusion
  89.5 29.3 %while.14 = (s32[]{:T(128)}, f32[4,512,512]{2,1,0:T(8,128)}, f32[4,512]{1,0:T(4,128)S(1)}, f32[]{:T(128)}, f32[]{:T(128)}, /*index=5*/bf16[4,512,128]{2,1,0:T(8,...) while((s32[]{:T(128)}, f32[4,512,512]{2,1,0:T(8,128)}, ...), condition=%wide.region_9.10_spmd, body=%wide.region_6.9_spmd.sunk | while | flops 1351546368 | bytes 19178136 | solution.py:90
  89.5 1.2 multiply_reduce_fusion.9
  91.0 2.8 exponential_convert_fusion.2
  93.8 2.3 fusion.147
  96.8 1.2 multiply_reduce_fusion.9
  98.3 2.8 exponential_convert_fusion.2
  101.1 2.3 fusion.147
  104.1 1.2 multiply_reduce_fusion.9
  105.7 2.8 exponential_convert_fusion.2
  108.5 2.3 fusion.147
  111.5 1.2 multiply_reduce_fusion.9
  113.0 2.8 exponential_convert_fusion.2
  115.8 2.3 fusion.147
  119.5 0.8 multiply_reduce_fusion.5
  120.4 118.6 %all-reduce.8.cloned.1.call-done = f32[2048,512]{1,0:T(8,128)} async-done(((f32[2048,512]{1,0:T(8,128)}), f32[2048,512]{1,0:T(8,128)}) %all-reduce.8.cloned.1.call-update) | async-done | bytes 4194320 | tf_op jit(solution)/shard_map/psum | solution.py:93
  239.0 1.8 fusion.7
  240.8 52.2 %all-gather.2.cloned.1.call-done = f32[2048,512]{1,0:T(8,128)} async-done(((f32[64,512]{1,0:T(8,128)}), f32[2048,512]{1,0:T(8,128)}) %all-gather.2.cloned.1.call-update) | async-done | bytes 4194320 | tf_op jit(solution)/shard_map/all_gather | solution.py:107
  293.0 2.3 slice.154
  295.3 1.6 copy.53
  296.8 1.1 broadcast_select_fusion
  299.8 66.2 %psum.38 = f32[2048]{0:T(1024)S(1)} all-reduce(f32[2048]{0:T(1024)S(1)} %bitcast.157), channel_id=1, replica_groups=mesh['dp'=32,'ind'=8] {'dp'}, use_global_device_ids=true, to_apply=%region_20.21 | all-reduce | flops 2048 | bytes 16384 | tf_op jit(solution)/shard_map/psum | solution.py:93
  366.7 63.7 %all-reduce.1 = f32[2048]{0:T(1024)S(1)} all-reduce(f32[2048]{0:T(1024)S(1)} %fusion.106), channel_id=1, replica_groups=mesh['dp'=32,'ind'=8] {'dp'}, use_global_device_ids=true, to_apply=%add.1 | all-reduce | flops 2048 | bytes 16384
  430.4 17.9 %psum.39 = f32[512]{0:T(512)S(1)} all-reduce(f32[512]{0:T(512)S(1)} %slice_select_fusion.1), channel_id=1, replica_groups=mesh['dp'=32,'ind'=8] {'ind'}, use_global_device_ids=true, to_apply=%region_21.22 | all-reduce | flops 512 | bytes 4096 | tf_op jit(solution)/shard_map/psum | solution.py:12
  448.4 1.6 copy.41
  449.9 1.5 fusion.31
  451.4 1.0 copy-done.2
  452.4 11.7 %cholesky.103 = f32[128,128]{1,0:T(8,128)S(1)} custom-call(f32[128,128]{1,0:T(8,128)S(1)} %cholesky.263), custom_call_target="Cholesky" | custom-call | tf_op jit(solution)/shard_map/jit(cholesky)/cholesky | solution.py:114
  464.2 9.8 %custom-call.32 = f32[1,128,128]{1,2,0:T(8,128)S(1)} custom-call(f32[1,128,128]{2,1,0:T(8,128)S(1)} %get-tuple-element.182), custom_call_target="InvertDiagBlocksLowerTriangular" | custom-call | tf_op jit(solution)/shard_map/jit(cholesky)/cholesky | solution.py:114
  474.0 1.2 fusion.50
  475.2 1.3 convolution_subtract_fusion
  476.5 11.7 %cholesky.215 = f32[128,128]{1,0:T(8,128)S(1)} custom-call(f32[128,128]{1,0:T(8,128)S(1)} %cholesky.267), custom_call_target="Cholesky" | custom-call | tf_op jit(solution)/shard_map/jit(cholesky)/cholesky | solution.py:114
  490.4 1.0 cholesky.222
  491.4 11.4 %custom-call.33 = f32[1,128,128]{1,2,0:T(8,128)} custom-call(f32[1,128,128]{2,1,0:T(8,128)} %get-tuple-element.180), custom_call_target="InvertDiagBlocksLowerTriangular" | custom-call | tf_op jit(solution)/shard_map/jit(cholesky)/cholesky | solution.py:114
  502.8 0.8 constant_dynamic-update-slice_fusion.2
  503.7 1.2 convolution_dynamic-update-slice_fusion
  504.8 1.5 convolution_subtract_fusion.1
  506.4 11.7 %cholesky.236 = f32[128,128]{1,0:T(8,128)S(1)} custom-call(f32[128,128]{1,0:T(8,128)S(1)} %cholesky.272), custom_call_target="Cholesky" | custom-call | tf_op jit(solution)/shard_map/jit(cholesky)/cholesky | solution.py:114
  518.1 1.1 select_reduce_fusion.1
  519.3 10.6 %custom-call.34 = f32[1,128,128]{1,2,0:T(8,128)S(1)} custom-call(f32[1,128,128]{2,1,0:T(8,128)} %get-tuple-element.178), custom_call_target="InvertDiagBlocksLowerTriangular" | custom-call | tf_op jit(solution)/shard_map/jit(cholesky)/cholesky | solution.py:114
  530.3 1.3 convolution_subtract_fusion.2
  531.6 11.9 %cholesky.253 = f32[128,128]{1,0:T(8,128)S(1)} custom-call(f32[128,128]{1,0:T(8,128)S(1)} %convolution_subtract_fusion.2), custom_call_target="Cholesky" | custom-call | tf_op jit(solution)/shard_map/jit(cholesky)/cholesky | solution.py:114
  543.7 1.4 compare_reduce_fusion.1
  549.0 2.4 fusion.32
  552.0 14.4 %while.15 = (s32[]{:T(128)}, f32[512,512]{0,1:T(8,128)}, s32[4,2]{0,1:T(2,128)S(1)}, f32[4,128,128]{2,1,0:T(8,128)}, s32[]{:T(128)}) while((s32[]{:T(128)}, f32[512,512]{0,1:T(8,128)}, s32[4,2]{0,1:T(2,128)S(1)}, f32[4,128,128]{2,1,0:T(8,128)}, s32[]{:T(128)}) %tuple.55), condition=%wide.while_cond, body=%wide.while_body.sunk | while | flops 2 | bytes 393829 | solution.py:119
  552.6 2.3 dynamic-slice.8
  556.2 2.3 dynamic-slice.8
  559.8 2.3 dynamic-slice.8
  563.4 2.2 dynamic-slice.8
  566.4 40.1 %custom-call.35 = f32[4,128,128]{1,2,0:T(8,128)S(1)} custom-call(f32[4,128,128]{2,1,0:T(8,128)} %get-tuple-element.102), custom_call_target="InvertDiagBlocksLowerTriangular" | custom-call | tf_op jit(solution)/shard_map/triangular_solve | solution.py:119
  606.9 1.0 fusion.10
  608.0 1.1 fusion.11
  609.3 1.2 fusion.14
  611.3 1.0 convolution_subtract_fusion.5
  612.5 1.1 convolution_subtract_fusion.4
  613.8 1.2 convolution_subtract_fusion.3
  615.2 4.5 gather_fusion
  620.5 1.4 fusion.12
  (119 shorter events, 21.4 us)
Async XLA Ops:
  7.2 3.3 copy-start
  7.2 77.6 %all-reduce.6.cloned.1.call-start = ((), (), s32[]{:S(2)}) async-start(), calls=%async_computation | async-start | bytes 262144 | tf_op jit(solution)/shard_map/psum | solution.py:12
  9.0 230.0 %all-reduce.8.cloned.1.call-start = ((), (), s32[]{:S(2)}) async-start(), calls=%async_computation.1 | async-start | bytes 8388608 | tf_op jit(solution)/shard_map/psum | solution.py:93
  10.5 2.1 copy-start.9
  10.5 30.5 %copy-start.10 = (s32[32]{0:T(128)S(1)}, s32[32]{0:T(128)}, u32[]{:S(2)}) copy-start(s32[32]{0:T(128)} %param.15) | copy-start | bytes 388
  10.5 32.7 %copy-start.8 = (bf16[2048]{0:T(1024)(128)(2,1)S(1)}, bf16[2048]{0:T(1024)(128)(2,1)}, u32[]{:S(2)}) copy-start(bf16[2048]{0:T(1024)(128)(2,1)} %param.14) | copy-start | bytes 12292
  89.5 4.3 copy-start.11
  96.8 4.3 copy-start.11
  104.1 4.3 copy-start.11
  111.5 4.3 copy-start.11
  118.8 120.2 %copy-start.5 = (bf16[512,128]{1,0:T(8,128)(2,1)S(1)}, bf16[512,128]{1,0:T(8,128)(2,1)}, u32[]{:S(2)}) copy-start(bf16[512,128]{1,0:T(8,128)(2,1)} %all-reduce.6.cloned.1.call-done) | copy-start | bytes 393220
  118.8 174.2 %all-gather.2.cloned.1.call-start = ((), (), s32[]{:S(2)}) async-start(), calls=%async_computation.2 | async-start | bytes 4325376 | tf_op jit(solution)/shard_map/all_gather | solution.py:107
  239.0 59.0 %copy-start.12 = (u32[256]{0:T(256)S(1)}, u32[256]{0:T(256)}, u32[]{:S(2)}) copy-start(u32[256]{0:T(256)} %constant.249) | copy-start | bytes 3076
  240.8 207.6 %all-reduce.10.cloned.1.call-start = ((), (), s32[]{:S(2)}) async-start(), calls=%async_computation.3 | async-start | bytes 2097152 | tf_op jit(solution)/shard_map/psum | solution.py:12
  366.0 0.6 copy-start.6
  451.4 1.0 copy-start.2
  504.8 101.7 %copy-start.4 = (f32[64,512]{1,0:T(8,128)S(1)}, f32[64,512]{1,0:T(8,128)}, u32[]{:S(2)}) copy-start(f32[64,512]{1,0:T(8,128)} %fusion.7) | copy-start | bytes 393220
  545.7 2.7 copy-start.1
  609.3 2.0 copy-start.7
  615.2 7.4 %copy-start.3 = (f32[64,512]{1,0:T(8,128)}, f32[64,512]{1,0:T(8,128)S(1)}, u32[]{:S(2)}) copy-start(f32[64,512]{1,0:T(8,128)S(1)} %pad_maximum_fusion) | copy-start | bytes 393220
Sparse Core Ops, SparseCore 0:
  10.9 73.8 all-reduce.5
  118.9 119.9 all-reduce.7
  242.1 50.8 all-gather.1
  298.1 75.4 all-reduce.9
where the time goes:
time: 638 us; the launch traced here: 630 us
  waiting for transfers between devices  212 us (33%)
  blocking collectives  175 us (27%)
  other arithmetic  143 us (22%)
  matrix products  47.9 us (8%)
  local copies, waits for them, and re-layouts  31.2 us (5%)
  between operations  21.6 us (3%)
    psum x1, waiting for transfers between devices, body(): gram_total, cross_total = lax.psum((gram_rows, cross_rows), 'dp')  119 us
    another operation x14, other arithmetic, body(): factor_top = jnp.linalg.cholesky(system_top)  83.5 us
    psum x1, blocking collectives, body(): gram_total, cross_total = lax.psum((gram_rows, cross_rows), 'dp')  66.2 us
    unnamed x1, blocking collectives  63.7 us
    all_gather x1, waiting for transfers between devices, body(): lax.all_gather(system_rows, 'dp', axis=0, tiled=True)  52.2 us
    another operation x4, other arithmetic, body(): lax.linalg.triangular_solve(factor_top, system_rows, left_side=False, low...  43 us
    psum x2, waiting for transfers between devices, from_root(): return lax.psum(jnp.where(mine, shard, jnp.zeros_like(shard)), axis)  40.8 us
    all_gather x1, blocking collectives, body(): embedded = lax.all_gather(embedded_piece, 'ind', axis=0, tiled=True)  27.6 us
  transfers between devices with their start and end apart: 4, of which 3 were waited for; matrix products, arithmetic and copies ran while one was open for 1% of the time, Pallas kernels for 0%

commit v1 on v0

--- a/solution.py
+++ b/solution.py
@@ -9,7 +9,7 @@
 
 def from_root(shard, axis, root):
     mine = lax.axis_index(axis) == root
-    return lax.psum(jnp.where(mine, shard, jnp.zeros_like(shard)), axis)
+    return jnp.sum(lax.all_gather(jnp.where(mine, shard, jnp.zeros_like(shard)), axis), axis=0)
 
 
 def embed(inputs, w_in, w_mid, w_out, feat_gain):

time: 638 us -> 605 us (0.948)
  waiting for transfers between devices: 212 us -> 177 us
  blocking collectives: 175 us -> 183 us
  local copies, waits for them, and re-layouts: 31.2 us -> 23.8 us
    psum x2 -> x0, waiting for transfers between devices: 40.8 us -> none  [from_root(): return lax.psum(jnp.where(mine, shard, jnp.zeros_like(shard)), axis)]
    all_gather x0 -> x1, blocking collectives: none -> 24.6 us  [from_root(): lax.all_gather(jnp.where(mine, shard, jnp.zeros_like(shard)), axis)]
    psum x1 -> x0, blocking collectives: 17.9 us -> none  [from_root(): return lax.psum(jnp.where(mine, shard, jnp.zeros_like(shard)), axis)]
    all_gather x0 -> x2, waiting for transfers between devices: none -> 6.64 us  [from_root(): lax.all_gather(jnp.where(mine, shard, jnp.zeros_like(shard)), axis)]
    another operation x24 -> x16, local copies, waits for them, and re-layouts: 14.4 us -> 14 us
where the time goes in v1:
time: 605 us; the launch traced here: 598 us
  blocking collectives  183 us (30%)
  waiting for transfers between devices  177 us (29%)
  other arithmetic  146 us (24%)
  matrix products  46 us (8%)
  local copies, waits for them, and re-layouts  23.8 us (4%)
  between operations  21.5 us (4%)
    psum x1, waiting for transfers between devices, body(): gram_total, cross_total = lax.psum((gram_rows, cross_rows), 'dp')  118 us
    another operation x14, other arithmetic, body(): factor_top = jnp.linalg.cholesky(system_top)  81.1 us
    psum x1, blocking collectives, body(): gram_total, cross_total = lax.psum((gram_rows, cross_rows), 'dp')  66.2 us
    unnamed x1, blocking collectives  63.7 us
    all_gather x1, waiting for transfers between devices, body(): lax.all_gather(system_rows, 'dp', axis=0, tiled=True)  52.2 us
    another operation x4, other arithmetic, body(): lax.linalg.triangular_solve(factor_top, system_rows, left_side=False, low...  43 us
    all_gather x1, blocking collectives, body(): embedded = lax.all_gather(embedded_piece, 'ind', axis=0, tiled=True)  28.1 us
    all_gather x1, blocking collectives, from_root(): lax.all_gather(jnp.where(mine, shard, jnp.zeros_like(shard)), axis)  24.6 us
  transfers between devices with their start and end apart: 4, of which 3 were waited for; matrix products, arithmetic and copies ran while one was open for 1% of the time, Pallas kernels for 0%

profile of v1, /device:TPU:0, one launch (start us, length us, event | category | flops | bytes accessed | tf_op | source)
XLA Modules:
  0.0 597.8 jit_solution(12315948905141605384)
XLA Ops:
  7.2 1.7 slice_select_fusion.1
  10.3 1.4 fusion.56
  11.8 2.1 multiply_reduce_fusion.4
  14.0 28.1 %all_gather.29 = bf16[2048,128]{0,1:T(8,128)(2,1)S(1)} all-gather(bf16[256,128]{0,1:T(8,128)(2,1)S(1)} %multiply_convert_fusion), channel_id=1, replica_groups=mesh['dp'=32,'ind'=8] {'ind'}, dimensions={0}, use_global_device_ids=true | all-gather | bytes 589824 | tf_op jit(solution)/shard_map/all_gather | solution.py:68
  42.5 0.7 fusion.91
  44.6 6.6 %all-gather.10.cloned.1.call-done = bf16[4096,128]{1,0:T(8,128)(2,1)} async-done(((bf16[512,128]{1,0:T(8,128)(2,1)}), bf16[4096,128]{1,0:T(8,128)(2,1)}) %all-gather.10.cloned.1.call-update) | async-done | bytes 1048592 | tf_op jit(solution)/shard_map/all_gather | solution.py:12
  51.2 1.4 reduce_sum.109
  52.7 2.7 select_convert_fusion
  55.4 29.3 %while.14 = (s32[]{:T(128)}, f32[4,512,512]{2,1,0:T(8,128)}, f32[4,512]{1,0:T(4,128)S(1)}, f32[]{:T(128)}, f32[]{:T(128)}, /*index=5*/bf16[4,512,128]{2,1,0:T(8,...) while((s32[]{:T(128)}, f32[4,512,512]{2,1,0:T(8,128)}, ...), condition=%wide.region_9.10_spmd, body=%wide.region_6.9_spmd.sunk | while | flops 1351546368 | bytes 19178136 | solution.py:90
  55.4 1.2 multiply_reduce_fusion.9
  57.0 2.8 exponential_convert_fusion.2
  59.7 2.3 fusion.147
  62.0 0.6 fusion.148
  62.7 1.2 multiply_reduce_fusion.9
  64.3 2.8 exponential_convert_fusion.2
  67.1 2.3 fusion.147
  70.1 1.2 multiply_reduce_fusion.9
  71.7 2.7 exponential_convert_fusion.2
  74.4 2.3 fusion.147
  77.4 1.2 multiply_reduce_fusion.9
  79.0 2.8 exponential_convert_fusion.2
  81.7 2.3 fusion.147
  84.0 0.7 fusion.148
  85.5 0.8 multiply_reduce_fusion.5
  86.3 118.2 %all-reduce.4.cloned.1.call-done = f32[2048,512]{1,0:T(8,128)} async-done(((f32[2048,512]{1,0:T(8,128)}), f32[2048,512]{1,0:T(8,128)}) %all-reduce.4.cloned.1.call-update) | async-done | bytes 4194320 | tf_op jit(solution)/shard_map/psum | solution.py:93
  204.5 1.8 fusion.7
  206.4 52.2 %all-gather.8.cloned.1.call-done = f32[2048,512]{1,0:T(8,128)} async-done(((f32[64,512]{1,0:T(8,128)}), f32[2048,512]{1,0:T(8,128)}) %all-gather.8.cloned.1.call-update) | async-done | bytes 4194320 | tf_op jit(solution)/shard_map/all_gather | solution.py:107
  258.6 2.4 slice_select_fusion
  262.8 66.2 %psum.15 = f32[2048]{0:T(1024)S(1)} all-reduce(f32[2048]{0:T(1024)S(1)} %bitcast.164), channel_id=1, replica_groups=mesh['dp'=32,'ind'=8] {'dp'}, use_global_device_ids=true, to_apply=%region_20.21 | all-reduce | flops 2048 | bytes 16384 | tf_op jit(solution)/shard_map/psum | solution.py:93
  329.7 63.7 %all-reduce.1 = f32[2048]{0:T(1024)S(1)} all-reduce(f32[2048]{0:T(1024)S(1)} %fusion.106), channel_id=1, replica_groups=mesh['dp'=32,'ind'=8] {'dp'}, use_global_device_ids=true, to_apply=%add.1 | all-reduce | flops 2048 | bytes 16384
  393.4 24.6 %all-gather.3 = f32[8,1,512]{2,1,0:T(1,128)S(1)} all-gather(f32[1,1,512]{2,1,0:T(1,128)S(1)} %bitcast.165), channel_id=4, replica_groups=mesh['dp'=32,'ind'=8] {'ind'}, dimensions={0}, use_global_device_ids=true | all-gather | bytes 18432 | tf_op jit(solution)/shard_map/all_gather | solution.py:12
  418.1 4.5 reduce_sum.114
  422.6 1.3 copy.22
  423.9 1.5 fusion.31
  425.4 1.0 copy-done.2
  426.4 11.7 %cholesky.103 = f32[128,128]{1,0:T(8,128)S(1)} custom-call(f32[128,128]{1,0:T(8,128)S(1)} %cholesky.263), custom_call_target="Cholesky" | custom-call | tf_op jit(solution)/shard_map/jit(cholesky)/cholesky | solution.py:114
  438.3 9.8 %custom-call.32 = f32[1,128,128]{1,2,0:T(8,128)S(1)} custom-call(f32[1,128,128]{2,1,0:T(8,128)S(1)} %get-tuple-element.184), custom_call_target="InvertDiagBlocksLowerTriangular" | custom-call | tf_op jit(solution)/shard_map/jit(cholesky)/cholesky | solution.py:114
  448.1 1.2 constant_dynamic-update-slice_fusion
  449.3 1.3 convolution_subtract_fusion
  451.2 12.7 %cholesky.215 = f32[128,128]{1,0:T(8,128)S(1)} custom-call(f32[128,128]{1,0:T(8,128)} %cholesky.267), custom_call_target="Cholesky" | custom-call | tf_op jit(solution)/shard_map/jit(cholesky)/cholesky | solution.py:114
  464.5 10.6 %custom-call.33 = f32[1,128,128]{1,2,0:T(8,128)S(1)} custom-call(f32[1,128,128]{2,1,0:T(8,128)} %get-tuple-element.181), custom_call_target="InvertDiagBlocksLowerTriangular" | custom-call | tf_op jit(solution)/shard_map/jit(cholesky)/cholesky | solution.py:114
  475.5 1.3 convolution_subtract_fusion.1
  476.8 11.7 %cholesky.236 = f32[128,128]{1,0:T(8,128)S(1)} custom-call(f32[128,128]{1,0:T(8,128)S(1)} %cholesky.272), custom_call_target="Cholesky" | custom-call | tf_op jit(solution)/shard_map/jit(cholesky)/cholesky | solution.py:114
  488.5 0.7 compare_reduce_fusion.1
  489.2 9.8 %custom-call.34 = f32[1,128,128]{1,2,0:T(8,128)S(1)} custom-call(f32[1,128,128]{2,1,0:T(8,128)S(1)} %get-tuple-element.178), custom_call_target="InvertDiagBlocksLowerTriangular" | custom-call | tf_op jit(solution)/shard_map/jit(cholesky)/cholesky | solution.py:114
  499.2 1.2 convolution_subtract_fusion.2
  500.4 11.9 %cholesky.253 = f32[128,128]{1,0:T(8,128)S(1)} custom-call(f32[128,128]{1,0:T(8,128)S(1)} %convolution_subtract_fusion.2), custom_call_target="Cholesky" | custom-call | tf_op jit(solution)/shard_map/jit(cholesky)/cholesky | solution.py:114
  512.4 0.8 compare_reduce_fusion
  516.5 2.4 fusion.32
  519.4 14.0 %while.15 = (s32[]{:T(128)}, f32[512,512]{1,0:T(8,128)}, s32[4,2]{0,1:T(2,128)S(1)}, f32[4,128,128]{2,1,0:T(8,128)}, s32[]{:T(128)}) while((s32[]{:T(128)}, f32[512,512]{1,0:T(8,128)}, s32[4,2]{0,1:T(2,128)S(1)}, f32[4,128,128]{2,1,0:T(8,128)}, s32[]{:T(128)}) %tuple.57), condition=%wide.while_cond, body=%wide.while_body.sunk | while | flops 2 | bytes 132705 | solution.py:119
  520.0 2.9 bitcast_dynamic-update-slice_fusion.2
  523.5 2.9 bitcast_dynamic-update-slice_fusion.2
  527.0 2.9 bitcast_dynamic-update-slice_fusion.2
  530.5 2.8 bitcast_dynamic-update-slice_fusion.2
  533.4 40.1 %custom-call.35 = f32[4,128,128]{1,2,0:T(8,128)S(1)} custom-call(f32[4,128,128]{2,1,0:T(8,128)} %get-tuple-element.102), custom_call_target="InvertDiagBlocksLowerTriangular" | custom-call | tf_op jit(solution)/shard_map/triangular_solve | solution.py:119
  573.8 1.0 fusion.10
  575.1 1.1 fusion.11
  576.4 1.2 fusion.14
  578.4 1.1 convolution_subtract_fusion.5
  579.7 1.2 convolution_subtract_fusion.4
  581.1 1.3 convolution_subtract_fusion.3
  582.6 4.5 gather_fusion
  587.1 0.7 log_reduce_fusion
  587.8 1.4 fusion.12
  (101 shorter events, 14.6 us)
Async XLA Ops:
  7.2 4.6 copy-start
  7.2 44.0 %all-gather.10.cloned.1.call-start = ((), (), s32[]{:S(2)}) async-start(), calls=%async_computation.2 | async-start | bytes 1179648 | tf_op jit(solution)/shard_map/all_gather | solution.py:12
  9.0 195.6 %all-reduce.4.cloned.1.call-start = ((), (), s32[]{:S(2)}) async-start(), calls=%async_computation | async-start | bytes 8388608 | tf_op jit(solution)/shard_map/psum | solution.py:93
  11.8 2.1 copy-start.8
  11.8 30.7 %copy-start.9 = (s32[32]{0:T(128)S(1)}, s32[32]{0:T(128)}, u32[]{:S(2)}) copy-start(s32[32]{0:T(128)} %param.15) | copy-start | bytes 388
  11.8 32.1 %copy-start.7 = (bf16[2048]{0:T(1024)(128)(2,1)S(1)}, bf16[2048]{0:T(1024)(128)(2,1)}, u32[]{:S(2)}) copy-start(bf16[2048]{0:T(1024)(128)(2,1)} %param.14) | copy-start | bytes 12292
  55.4 4.3 copy-start.10
  62.7 4.3 copy-start.10
  70.1 4.3 copy-start.10
  77.4 4.3 copy-start.10
  84.7 176.3 %copy-start.11 = (u32[256]{0:T(256)S(1)}, u32[256]{0:T(256)}, u32[]{:S(2)}) copy-start(u32[256]{0:T(256)} %constant.250) | copy-start | bytes 3076
  84.8 173.8 %all-gather.8.cloned.1.call-start = ((), (), s32[]{:S(2)}) async-start(), calls=%async_computation.1 | async-start | bytes 4325376 | tf_op jit(solution)/shard_map/all_gather | solution.py:107
  206.3 211.7 %all-gather.12.cloned.1.call-start = ((), (), s32[]{:S(2)}) async-start(), calls=%async_computation.3 | async-start | bytes 9437184 | tf_op jit(solution)/shard_map/all_gather | solution.py:12
  329.0 0.6 copy-start.5
  425.4 1.0 copy-start.2
  438.1 135.4 %copy-start.4 = (f32[64,512]{1,0:T(8,128)S(1)}, f32[64,512]{1,0:T(8,128)}, u32[]{:S(2)}) copy-start(f32[64,512]{1,0:T(8,128)} %fusion.7) | copy-start | bytes 393220
  512.3 4.1 copy-start.1
  576.4 2.0 copy-start.6
  582.6 7.4 %copy-start.3 = (f32[64,512]{1,0:T(8,128)}, f32[64,512]{1,0:T(8,128)S(1)}, u32[]{:S(2)}) copy-start(f32[64,512]{1,0:T(8,128)S(1)} %pad_maximum_fusion) | copy-start | bytes 393220
Sparse Core Ops, SparseCore 0:
  10.3 40.7 all-gather.9
  84.9 119.6 all-reduce.3
  207.7 50.8 all-gather.7
  261.1 93.5 all-gather.11
